TPU v7x, 256 devices: a whole 4x4x8 slice. The times are simulated.
256 devices in a mesh: crop: 2 (over y_hi), rows: 16 (over y_lo, x, core), hid: 8 (over z).
Axes of the slice: x: 4, y: 4 (y_hi: 2, y_lo: 2; y = y_hi * 2 + y_lo), z: 8, core: 2. Of those that a mesh axis runs over, the one named last changes fastest.
Arguments:
- tokens: bfloat16 [2, 32, 64, 4096], P('crop', 'rows', None, 'hid'), may hold values from -6 to 6
- cotangent: bfloat16 [2, 32, 64, 4096], P('crop', 'rows', None, 'hid'), may hold values from -6 to 6
- weight_in: bfloat16 [256, 64, 5, 256], P('rows', 'hid'), may hold values from -0.15625 to 0.15625
- weight_out: bfloat16 [256, 64, 5, 256], P('rows', 'hid'), may hold values from -0.078125 to 0.078125
- mix_kernel: float32 [9, 16384], P(None, 'hid'), may hold values from -4 to 4
- block_rows: int32 [64, 5], P('hid'), may hold values from 0 to 15, as said below
Outputs:
- grad_tokens: bfloat16 [2, 32, 64, 4096], P('crop', 'rows', None, 'hid')
- grad_w_in: float32 [256, 64, 5, 256], P(('crop', 'rows'), 'hid')
- grad_w_out: float32 [256, 64, 5, 256], P(('crop', 'rows'), 'hid')
- grad_kernel: float32 [9, 16384], P(None, 'hid')
Inputs may be any that keep to these rules, and one draw needn't show every extreme that they name: In each block column c, block_rows[c, 0] is a label L and block_rows[c, k] for k >= 1 is L with bit k - 1 flipped, so the 5 entries of a column differ; every value is the label of equally many block columns.
All inputs are finite; a program needn't handle non-finite values.
Results may differ from a plain program's by a relative error of at most 0.019.
Values may be sent and summed in bfloat16 or wider, within the bound.
No kernel may reach another device: no remote copies, remote signals or barrier semaphores. Data moves between devices by JAX's collectives and lax.ppermute only.
A program may use at most 128 MiB of HBM per device.

v0:
```python
import jax
import jax.numpy as jnp
from jax import lax
from jax.sharding import PartitionSpec as P

root_two_pi = 0.7978845608
cubic_coef = 0.044715
loss_scale = 0.03125


def padded(shard, sides, width):
    for axis, dim in sides:
        devices, length = (lax.axis_size(axis), shard.shape[dim])
        up = [(i, (i + 1) % devices) for i in range(devices - 1)]
        down = [(j, i) for i, j in up]
        last = lax.slice_in_dim(shard, length - width, length, axis=dim)
        initial = lax.slice_in_dim(shard, 0, width, axis=dim)
        before = lax.ppermute(last, axis, up)
        after = lax.ppermute(initial, axis, down)
        shard = jnp.concatenate([before, shard, after], axis=dim)
    return shard


def gelu_pair(preact):
    inner = root_two_pi * (preact + cubic_coef * preact * preact * preact)
    tanh_val = jnp.tanh(inner)
    gelu_out = 0.5 * preact * (1.0 + tanh_val)
    slopes = 0.5 * (1.0 + tanh_val) + 0.5 * preact * (1.0 - tanh_val * tanh_val) * root_two_pi * (
        1.0 + 3.0 * cubic_coef * preact * preact
    )
    return (gelu_out, slopes)


def on_device(tokens, cotangent, weight_in, weight_out, mix_kernel, block_rows):
    in_panel, out_panel = (
        lax.all_gather(weight_in, "rows", axis=0, tiled=True),
        lax.all_gather(weight_out, "rows", axis=0, tiled=True),
    )
    tok_full, cot_full = (
        lax.all_gather(tokens, "hid", axis=3, tiled=True),
        lax.all_gather(cotangent, "hid", axis=3, tiled=True),
    )
    crop_count, height, grid_width, depth_all = tok_full.shape
    tok_count = crop_count * height * grid_width
    block_size = in_panel.shape[0]
    col_count = in_panel.shape[1]
    nnz_count = in_panel.shape[2]
    block_count = depth_all // block_size
    hidden_local = col_count * block_size
    flat_rows = block_rows.reshape(-1)
    in_select = jnp.take(
        tok_full.reshape(tok_count, block_count, block_size), flat_rows, axis=1
    ).reshape(tok_count, col_count, nnz_count, block_size)
    grad_select = jnp.take(
        cot_full.reshape(tok_count, block_count, block_size), flat_rows, axis=1
    ).reshape(tok_count, col_count, nnz_count, block_size)
    pre_act = jnp.einsum("tckb,bcke->tce", in_select, in_panel, preferred_element_type=jnp.float32)
    gelu_out, slopes = gelu_pair(pre_act)
    active = gelu_out.astype(jnp.bfloat16).reshape(crop_count, height, grid_width, hidden_local)
    act_rim = padded(active, (("rows", 1),), 1)
    mix_grad = (
        jnp.einsum("tckd,fckd->tcf", grad_select, out_panel, preferred_element_type=jnp.float32)
        .astype(jnp.bfloat16)
        .reshape(crop_count, height, grid_width, hidden_local)
    )
    grad_rim = padded(mix_grad, (("rows", 1),), 1)
    act_pad = jnp.pad(act_rim.astype(jnp.float32), ((0, 0), (0, 0), (1, 1), (0, 0)))
    grad_pad = jnp.pad(grad_rim.astype(jnp.float32), ((0, 0), (0, 0), (1, 1), (0, 0)))
    grad_grid = mix_grad.astype(jnp.float32)
    mix_sum = jnp.zeros((crop_count, height, grid_width, hidden_local), jnp.float32)
    act_grad = jnp.zeros((crop_count, height, grid_width, hidden_local), jnp.float32)
    kern_terms = []
    for row_off in range(3):
        for col_off in range(3):
            tap = mix_kernel[3 * row_off + col_off]
            shifted = act_pad[:, row_off : row_off + height, col_off : col_off + grid_width]
            mix_sum = mix_sum + tap * shifted
            act_grad = (
                act_grad
                + tap
                * grad_pad[
                    :, 2 - row_off : 2 - row_off + height, 2 - col_off : 2 - col_off + grid_width
                ]
            )
            kern_terms.append(jnp.sum(shifted * grad_grid, axis=(0, 1, 2)))
    kern_local = jnp.stack(kern_terms, axis=0) * loss_scale
    mix_out = mix_sum.astype(jnp.bfloat16).reshape(tok_count, col_count, block_size)
    pre_grad = (act_grad.reshape(tok_count, col_count, block_size) * slopes).astype(jnp.bfloat16)
    kern_total = lax.psum(kern_local.astype(jnp.bfloat16), ("crop", "rows")).astype(jnp.float32)
    back_select = jnp.einsum(
        "tce,bcke->tckb", pre_grad, in_panel, preferred_element_type=jnp.float32
    )
    one_hot = (
        block_rows[:, :, None] == jnp.arange(block_count, dtype=jnp.int32)[None, None, :]
    ).astype(jnp.float32)
    token_terms = jnp.einsum(
        "tckb,ckr->trb", back_select, one_hot, precision=lax.Precision.HIGHEST
    ).reshape(crop_count, height, grid_width, depth_all)
    grad_tokens = lax.psum_scatter(
        token_terms.astype(jnp.bfloat16), "hid", scatter_dimension=3, tiled=True
    )
    first_term = jnp.einsum(
        "tckb,tce->bcke", in_select, pre_grad, preferred_element_type=jnp.float32
    )
    second_term = jnp.einsum(
        "tcf,tckd->fckd", mix_out, grad_select, preferred_element_type=jnp.float32
    )
    share_sums = lax.psum_scatter(
        (jnp.stack([first_term, second_term], axis=1) * loss_scale).astype(jnp.bfloat16),
        ("crop", "rows"),
        scatter_dimension=0,
        tiled=True,
    ).astype(jnp.float32)
    return (grad_tokens, share_sums[:, 0], share_sums[:, 1], kern_total)


def solution(mesh):
    placed = (
        P("crop", "rows", None, "hid"),
        P("crop", "rows", None, "hid"),
        P("rows", "hid", None, None),
        P("rows", "hid", None, None),
        P(None, "hid"),
        P("hid", None),
    )
    return jax.shard_map(
        on_device,
        mesh=mesh,
        in_specs=placed,
        out_specs=(
            P("crop", "rows", None, "hid"),
            P(("crop", "rows"), "hid", None, None),
            P(("crop", "rows"), "hid", None, None),
            P(None, "hid"),
        ),
        check_vma=False,
    )
```

profile of v0, /device:TPU:4, one launch (start us, length us, event | category | flops | bytes accessed | tf_op | source)
XLA Modules:
  0.0 380.4 jit_solution(11429003799002727429)
XLA Ops:
  7.2 0.7 all-gather.9.cloned.1.call-update
  7.9 0.7 all-gather.5.cloned.1.call-update
  8.7 1.8 copy.46
  10.5 1.8 copy.49
  12.4 0.8 reshape.183
  13.2 38.3 %all-gather.9.cloned.1.call-done = bf16[1,2,64,4096]{3,2,1,0:T(8,128)(2,1)} async-done(((bf16[1,2,64,512]{3,2,1,0:T(8,128)(2,1)}), bf16[1,2,64,4096]{3,2,1,0:T(8,128)(2,1)}) %all-gather.9.cloned.1.call-update) | async-done | bytes 1048592 | tf_op jit(solution)/shard_map/all_gather | solution.py:40
  51.5 1.5 copy.70
  53.0 0.3 copy.48
  53.3 37.1 %all-gather.5.cloned.1.call-done = bf16[1,2,64,4096]{3,2,1,0:T(8,128)(2,1)} async-done(((bf16[1,2,64,512]{3,2,1,0:T(8,128)(2,1)}), bf16[1,2,64,4096]{3,2,1,0:T(8,128)(2,1)}) %all-gather.5.cloned.1.call-update) | async-done | bytes 1048592 | tf_op jit(solution)/shard_map/all_gather | solution.py:41
  90.4 1.5 copy.68
  91.9 0.3 copy.45
  92.2 2.4 gather_fusion.1
  94.6 2.4 gather_fusion
  97.0 4.6 %broadcast_select_fusion.1 = (bf16[40,128,256]{2,1,0:T(8,128)(2,1)S(1)}, bf16[40,128,256]{2,1,0:T(8,128)(2,1)}) fusion(bf16[40,128,256]{2,1,0:T(8,128)(2,1)} %gather_fusion, pred[40]{0:T(512)(128)(4,1)S(1)} %compare_and_fusion, bf16[40,128,256]{2,1,0:T(8,128)(2,1)} %gather_fusion.1), kind=kLoop, calls=%fused_computation.18 | loop fusion | flops 2621440 | bytes 10485800 | tf_op jit(solution)/shard_map/jit(_take)/select_n | solution.py:54
  101.6 30.2 %all-gather.7.cloned.1.call-done = bf16[256,8,5,256]{3,0,2,1:T(8,128)(2,1)} async-done(((bf16[16,8,5,256]{3,0,2,1:T(8,128)(2,1)}), bf16[256,8,5,256]{3,0,2,1:T(8,128)(2,1)}) %all-gather.7.cloned.1.call-update) | async-done | bytes 5242896 | tf_op jit(solution)/shard_map/all_gather | solution.py:37
  131.8 4.3 %fusion.9 = bf16[128,8,256]{2,0,1:T(8,128)(2,1)S(1)} fusion(bf16[128,8,5,256]{3,0,2,1:T(8,128)(2,1)S(1)} %bitcast.97, bf16[256,8,5,256]{3,0,2,1:T(8,128)(2,1)} %all-gather.7.cloned.1.call-done), kind=kOutput, calls=%fused_computation.39 | convolution fusion | flops 671350784 | bytes 8388608 | tf_op jit(solution)/shard_map/tckd,fckd->tcf/dot_general | solution.py:62
  136.2 1.1 copy.47
  137.2 1.3 reshape.185
  138.6 2.1 collective-permute-start
  140.7 3.4 collective-permute-start.1
  144.2 2.0 collective-permute-done
  146.3 3.6 collective-permute-done.1
  150.0 0.9 fusion.25
  150.9 1.3 copy.69
  152.2 25.9 %all-gather.11.cloned.1.call-done = bf16[256,8,5,256]{3,0,2,1:T(8,128)(2,1)} async-done(((bf16[16,8,5,256]{3,0,2,1:T(8,128)(2,1)}), bf16[256,8,5,256]{3,0,2,1:T(8,128)(2,1)}) %all-gather.11.cloned.1.call-update) | async-done | bytes 5242896 | tf_op jit(solution)/shard_map/all_gather | solution.py:36
  178.1 5.1 %multiply_convert_fusion = (bf16[128,8,256]{2,0,1:T(8,128)(2,1)S(1)}, bf16[128,8,256]{2,0,1:T(8,128)(2,1)}) fusion(f32[128,8,256]{2,1,0:T(8,128)} %bitcast.108, bf16[128,8,5,256]{3,0,2,1:T(8,128)(2,1)S(1)} %bitcast.99, bf16[256,8,5,256]{3,0,2,1:T(8,128)(2,1)} %all-gather.11.cloned.1.call-done), kind=kOutput, calls=%fused_computation.76 | convolution fusion | flops 676593664 | bytes 9961472 | tf_op jit(solution)/shard_map/tckb,bcke->tce/dot_general | solution.py:57
  183.3 1.1 copy.53
  184.4 2.1 reshape.189
  186.5 1.1 fusion.46
  187.5 2.1 collective-permute-start.2
  189.7 3.6 collective-permute-start.3
  193.3 2.7 convolution_bitcast_fusion.1
  196.0 1.0 collective-permute-done.3
  197.2 0.9 add_convert_fusion
  198.2 0.7 copy-done.1
  198.9 1.6 convolution_bitcast_fusion
  200.5 5.7 %fusion = bf16[256,2,8,5,256]{0,4,3,2,1:T(8,128)(2,1)} fusion(f32[256,1,8,5,256]{0,4,3,2,1:T(8,128)S(1)} %convolution_bitcast_fusion, f32[256,1,8,5,256]{0,4,3,2,1:T(8,128)S(1)} %convolution_bitcast_fusion.1), kind=kLoop, calls=%fused_computation.3 | loop fusion | flops 15728640 | bytes 31457280 | tf_op jit(solution)/shard_map/convert_element_type | solution.py:109
  206.2 15.4 %copy.56 = bf16[256,2,8,5,256]{4,2,3,1,0:T(8,128)(2,1)} copy(bf16[256,2,8,5,256]{0,4,3,2,1:T(8,128)(2,1)} %fusion) | data formatting | bytes 20971520 | tf_op jit(solution)/shard_map/convert_element_type | solution.py:109
  221.9 0.4 copy-done.6
  222.6 4.3 %convolution_bitcast_fusion.2 = f32[128,8,5,256]{3,0,2,1:T(8,128)S(1)} fusion(bf16[256,8,5,256]{3,0,2,1:T(8,128)(2,1)} %all-gather.11.cloned.1.call-done, bf16[128,8,256]{2,0,1:T(8,128)(2,1)S(1)} %copy-done.4), kind=kOutput, calls=%fused_computation.19 | convolution fusion | flops 671088640 | bytes 11010048 | tf_op jit(solution)/shard_map/tce,bcke->tckb/dot_general | solution.py:90
  227.0 5.9 %fusion.5 = bf16[128,16,256]{2,1,0:T(8,128)(2,1)} fusion(f32[128,8,5,256]{3,0,2,1:T(8,128)S(1)} %convolution_bitcast_fusion.2, s32[8,5]{0,1:T(8,128)S(1)} %copy.44), kind=kOutput, calls=%fused_computation.35 | convolution fusion | flops 252183168 | bytes 6291616 | tf_op jit(solution)/shard_map/tckb,ckr->trb/dot_general | solution.py:96
  232.8 2.3 convert_element_type.87
  235.2 1.0 fusion.39
  236.4 117.1 %psum.7 = bf16[9,2048]{1,0:T(8,128)(2,1)S(1)} all-reduce(bf16[9,2048]{1,0:T(8,128)(2,1)S(1)} %multiply_convert_fusion.1), channel_id=1, replica_groups=mesh['crop'=2,'rows'=16,'hid'=8] {'crop','rows'}, use_global_device_ids=true, to_apply=%region_11.13 | all-reduce | flops 18432 | bytes 73728 | tf_op jit(solution)/shard_map/psum | solution.py:89
  353.5 0.7 convert_element_type.95
  354.2 1.0 convert_element_type.92
  355.2 0.9 slice_bitcast_fusion
  356.1 17.5 %reduce-scatter.3.cloned.1.call-done = bf16[1,2,64,512]{3,2,1,0:T(8,128)(2,1)} async-done(((bf16[1,2,64,4096]{3,2,1,0:T(8,128)(2,1)}), bf16[1,2,64,512]{3,2,1,0:T(8,128)(2,1)}) %reduce-scatter.3.cloned.1.call-update) | async-done | bytes 131088 | tf_op jit(solution)/shard_map/reduce_scatter | solution.py:99
  (35 shorter events, 1.6 us)
Async XLA Ops:
  7.2 44.3 %all-gather.9.cloned.1.call-start = ((), (), s32[]{:S(2)}) async-start(), calls=%async_computation.4 | async-start | bytes 1179648 | tf_op jit(solution)/shard_map/all_gather | solution.py:40
  7.9 82.5 %all-gather.5.cloned.1.call-start = ((), (), s32[]{:S(2)}) async-start(), calls=%async_computation.2 | async-start | bytes 1179648 | tf_op jit(solution)/shard_map/all_gather | solution.py:41
  8.6 123.2 %all-gather.7.cloned.1.call-start = ((), (), s32[]{:S(2)}) async-start(), calls=%async_computation.3 | async-start | bytes 5570560 | tf_op jit(solution)/shard_map/all_gather | solution.py:37
  10.5 167.7 %all-gather.11.cloned.1.call-start = ((), (), s32[]{:S(2)}) async-start(), calls=%async_computation.5 | async-start | bytes 5570560 | tf_op jit(solution)/shard_map/all_gather | solution.py:36
  12.3 341.8 %reduce-scatter.5.cloned.1.call-start = ((), (), s32[]{:S(2)}) async-start(), calls=%async_computation.7 | async-start | bytes 10813440 | tf_op jit(solution)/shard_map/reduce_scatter | solution.py:108
  101.6 34.5 %copy-start = (bf16[40,128,256]{2,1,0:T(8,128)(2,1)}, bf16[40,128,256]{2,1,0:T(8,128)(2,1)S(1)}, u32[]{:S(2)}) copy-start(bf16[40,128,256]{2,1,0:T(8,128)(2,1)S(1)} %get-tuple-element.43) | copy-start | bytes 7864324
  136.1 8.0 %copy-start.5 = (f32[9,2048]{1,0:T(8,128)S(1)}, f32[9,2048]{1,0:T(8,128)}, u32[]{:S(2)}) copy-start(f32[9,2048]{1,0:T(8,128)} %param.12) | copy-start | bytes 221188
  138.6 7.7 %collective-permute-start = (bf16[1,1,64,2048]{3,2,1,0:T(8,128)(2,1)S(1)}, bf16[1,1,64,2048]{3,2,1,0:T(8,128)(2,1)S(1)}, u32[]{:S(2)}, u32[]{:S(2)}) collective-permute-start(bf16[1,1,64,2048]{3,2,1,0:T(8,128)(2,1)S(1)} %get-tuple-element.32), channel_id=1, source_target_pairs={{0,8},{8,16},{16,24},{24,32},{32,40},{40,48},{48,56},{56,64},{64,7... | collective-permute-start | bytes 786440 | tf_op jit(solution)/shard_map/ppermute | solution.py:18
  140.7 9.2 %collective-permute-start.1 = (bf16[1,1,64,2048]{3,2,1,0:T(8,128)(2,1)S(1)}, bf16[1,1,64,2048]{3,2,1,0:T(8,128)(2,1)S(1)}, u32[]{:S(2)}, u32[]{:S(2)}) collective-permute-start(bf16[1,1,64,2048]{3,2,1,0:T(8,128)(2,1)S(1)} %get-tuple-element.33), channel_id=1, source_target_pairs={{8,0},{16,8},{24,16},{32,24},{40,32},{48,40},{56,48},{64,56},{72,6... | collective-permute-start | bytes 786440 | tf_op jit(solution)/shard_map/ppermute | solution.py:19
  150.0 28.1 %copy-start.2 = (bf16[40,128,256]{2,1,0:T(8,128)(2,1)S(1)}, bf16[40,128,256]{2,1,0:T(8,128)(2,1)}, u32[]{:S(2)}) copy-start(bf16[40,128,256]{2,1,0:T(8,128)(2,1)} %get-tuple-element.44) | copy-start | bytes 7864324
  187.5 8.4 %collective-permute-start.2 = (bf16[1,1,64,2048]{3,2,1,0:T(8,128)(2,1)S(1)}, bf16[1,1,64,2048]{3,2,1,0:T(8,128)(2,1)S(1)}, u32[]{:S(2)}, u32[]{:S(2)}) collective-permute-start(bf16[1,1,64,2048]{3,2,1,0:T(8,128)(2,1)S(1)} %get-tuple-element.30), channel_id=1, source_target_pairs={{0,8},{8,16},{16,24},{24,32},{32,40},{40,48},{48,56},{56,64},{64,7... | collective-permute-start | bytes 786440 | tf_op jit(solution)/shard_map/ppermute | solution.py:18
  189.7 7.3 %collective-permute-start.3 = (bf16[1,1,64,2048]{3,2,1,0:T(8,128)(2,1)S(1)}, bf16[1,1,64,2048]{3,2,1,0:T(8,128)(2,1)S(1)}, u32[]{:S(2)}, u32[]{:S(2)}) collective-permute-start(bf16[1,1,64,2048]{3,2,1,0:T(8,128)(2,1)S(1)} %get-tuple-element.31), channel_id=1, source_target_pairs={{8,0},{16,8},{24,16},{32,24},{40,32},{48,40},{56,48},{64,56},{72,6... | collective-permute-start | bytes 786440 | tf_op jit(solution)/shard_map/ppermute | solution.py:19
  193.3 3.7 copy-start.3
  197.2 1.7 copy-start.1
  221.6 0.7 copy-start.6
  221.6 1.1 copy-start.4
  221.6 152.0 %reduce-scatter.3.cloned.1.call-start = ((), (), s32[]{:S(2)}) async-start(), calls=%async_computation.6 | async-start | bytes 1179648 | tf_op jit(solution)/shard_map/reduce_scatter | solution.py:99
Sparse Core Ops, SparseCore 0:
  9.8 41.6 all-gather.8
  53.3 37.0 all-gather.4
  92.8 39.0 all-gather.6
  134.0 44.0 all-gather.10
  221.7 110.2 reduce-scatter.4
  335.1 38.3 reduce-scatter.2
where the time goes:
time: 381 us; the launch traced here: 380 us
  waiting for transfers between devices  157 us (41%)
  blocking collectives  117 us (31%)
  local copies, waits for them, and re-layouts  41.1 us (11%)
  matrix products  23.8 us (6%)
  other arithmetic  15.2 us (4%)
  between operations  14.3 us (4%)
  starting transfers between devices  11.8 us (3%)
    psum x1, blocking collectives, on_device(): lax.psum(kern_local.astype(jnp.bfloat16), ('crop', 'rows'))  117 us
    all_gather x1, waiting for transfers between devices, on_device(): lax.all_gather(tokens, 'hid', axis=3, tiled=True)  38.3 us
    all_gather x1, waiting for transfers between devices, on_device(): lax.all_gather(cotangent, 'hid', axis=3, tiled=True)  37.1 us
    all_gather x1, waiting for transfers between devices, on_device(): lax.all_gather(weight_out, 'rows', axis=0, tiled=True)  30.2 us
    all_gather x1, waiting for transfers between devices, on_device(): lax.all_gather(weight_in, 'rows', axis=0, tiled=True)  25.9 us
    reduce_scatter x1, waiting for transfers between devices, on_device(): lax.psum_scatter(token_terms.astype(jnp.bfloat16), 'hid', scatter_dimensi...  17.5 us
    convert_element_type x1, local copies, waits for them, and re-layouts, on_device(): (jnp.stack([first_term, second_term], axis=1) * loss_scale).astype(jnp.bf...  15.4 us
    unnamed x21, local copies, waits for them, and re-layouts  9.42 us
  transfers between devices with their start and end apart: 10, of which 8 were waited for; matrix products, arithmetic and copies ran while one was open for 12% of the time, Pallas kernels for 0%

commit v1 on v0

--- a/solution.py
+++ b/solution.py
@@ -36,8 +36,21 @@
         lax.all_gather(weight_in, "rows", axis=0, tiled=True),
         lax.all_gather(weight_out, "rows", axis=0, tiled=True),
     )
+
+    def store_rounds(buf, array_axis):
+        state_next = jnp.concatenate(
+            jax.lax.all_to_all(
+                jnp.stack([buf for _ in range(jax.lax.axis_size("hid"))]),
+                concat_axis=0,
+                split_axis=0,
+                axis_name="hid",
+            ),
+            array_axis,
+        )
+        return state_next
+
     tok_full, cot_full = (
-        lax.all_gather(tokens, "hid", axis=3, tiled=True),
+        store_rounds(tokens, 3),
         lax.all_gather(cotangent, "hid", axis=3, tiled=True),
     )
     crop_count, height, grid_width, depth_all = tok_full.shape

time: 381 us -> 352 us (0.924)
  waiting for transfers between devices: 157 us -> 117 us
  starting transfers between devices: 11.8 us -> 20 us
    all_gather x1 -> x0, waiting for transfers between devices: 38.3 us -> none  [on_device(): lax.all_gather(tokens, 'hid', axis=3, tiled=True)]
    all_to_all x0 -> x1, starting transfers between devices: none -> 8.47 us  [store_rounds(): jax.lax.all_to_all(jnp.stack([buf for _ in range(jax.lax.axis_size('hid')...]
    another operation x0 -> x3, local copies, waits for them, and re-layouts: none -> 4.78 us  [the longest x2 2.77 us: on_device(): tok_full.reshape(tok_count, block_count, block_size)]
    unnamed x21 -> x20, local copies, waits for them, and re-layouts: 9.42 us -> 8.16 us
  transfers between devices with their start and end apart: 10 -> 10, of which waited for: 8 -> 7; matrix products, arithmetic and copies ran while one was open for 12% -> 14% of each run, Pallas kernels for 0% -> 0%
where the time goes in v1:
time: 352 us; the launch traced here: 351 us
  waiting for transfers between devices  117 us (33%)
  blocking collectives  117 us (33%)
  local copies, waits for them, and re-layouts  44.1 us (13%)
  matrix products  23.8 us (7%)
  starting transfers between devices  20 us (6%)
  other arithmetic  15.1 us (4%)
  between operations  14 us (4%)
    psum x1, blocking collectives, on_device(): lax.psum(kern_local.astype(jnp.bfloat16), ('crop', 'rows'))  117 us
    all_gather x1, waiting for transfers between devices, on_device(): lax.all_gather(cotangent, 'hid', axis=3, tiled=True)  38 us
    all_gather x1, waiting for transfers between devices, on_device(): lax.all_gather(weight_out, 'rows', axis=0, tiled=True)  28.2 us
    all_gather x1, waiting for transfers between devices, on_device(): lax.all_gather(weight_in, 'rows', axis=0, tiled=True)  26.4 us
    reduce_scatter x1, waiting for transfers between devices, on_device(): lax.psum_scatter(token_terms.astype(jnp.bfloat16), 'hid', scatter_dimensi...  17.5 us
    convert_element_type x1, local copies, waits for them, and re-layouts, on_device(): (jnp.stack([first_term, second_term], axis=1) * loss_scale).astype(jnp.bf...  15.4 us
    all_to_all x1, starting transfers between devices, store_rounds(): jax.lax.all_to_all(jnp.stack([buf for _ in range(jax.lax.axis_size('hid')...  8.47 us
    unnamed x20, local copies, waits for them, and re-layouts  8.16 us
  transfers between devices with their start and end apart: 10, of which 7 were waited for; matrix products, arithmetic and copies ran while one was open for 14% of the time, Pallas kernels for 0%

profile of v1, /device:TPU:4, one launch (start us, length us, event | category | flops | bytes accessed | tf_op | source)
XLA Modules:
  0.0 351.3 jit_solution(7625391671693953295)
XLA Ops:
  7.2 0.7 all-gather.4.cloned.1.call-update
  8.0 1.8 copy.46
  9.8 1.8 copy.50
  11.6 2.0 stack.50
  13.6 8.5 %all-to-all-start = ((bf16[8,1,2,64,512]{4,3,2,1,0:T(8,128)(2,1)}), bf16[8,1,2,64,512]{4,3,2,1,0:T(8,128)(2,1)S(1)}, u32[]{:S(2)}, u32[]{:S(2)}) async-start(bf16[8,1,2,64,512]{4,3,2,1,0:T(8,128)(2,1)} %stack.50), calls=%async_computation | async-start | bytes 2097152 | tf_op jit(solution)/shard_map/all_to_all | solution.py:42
  22.2 38.0 %all-gather.4.cloned.1.call-done = bf16[1,2,64,4096]{3,2,1,0:T(8,128)(2,1)} async-done(((bf16[1,2,64,512]{3,2,1,0:T(8,128)(2,1)}), bf16[1,2,64,4096]{3,2,1,0:T(8,128)(2,1)}) %all-gather.4.cloned.1.call-update) | async-done | bytes 1048592 | tf_op jit(solution)/shard_map/all_gather | solution.py:54
  60.2 1.5 copy.69
  61.7 0.3 copy.45
  62.0 0.6 copy.48
  62.6 1.2 reshape_reshape.3
  63.8 1.6 copy.49
  65.4 2.4 gather_fusion.1
  67.8 2.4 gather_fusion
  70.2 4.6 %broadcast_select_fusion.1 = (bf16[40,128,256]{2,1,0:T(8,128)(2,1)S(1)}, bf16[40,128,256]{2,1,0:T(8,128)(2,1)}) fusion(bf16[40,128,256]{2,1,0:T(8,128)(2,1)} %gather_fusion, pred[40]{0:T(512)(128)(4,1)S(1)} %compare_and_fusion, bf16[40,128,256]{2,1,0:T(8,128)(2,1)} %gather_fusion.1), kind=kLoop, calls=%fused_computation.18 | loop fusion | flops 2621440 | bytes 10485800 | tf_op jit(solution)/shard_map/jit(_take)/select_n | solution.py:67
  74.8 28.2 %all-gather.6.cloned.1.call-done = bf16[256,8,5,256]{3,0,2,1:T(8,128)(2,1)} async-done(((bf16[16,8,5,256]{3,0,2,1:T(8,128)(2,1)}), bf16[256,8,5,256]{3,0,2,1:T(8,128)(2,1)}) %all-gather.6.cloned.1.call-update) | async-done | bytes 5242896 | tf_op jit(solution)/shard_map/all_gather | solution.py:37
  103.0 4.3 %fusion.9 = bf16[128,8,256]{2,0,1:T(8,128)(2,1)S(1)} fusion(bf16[128,8,5,256]{3,0,2,1:T(8,128)(2,1)S(1)} %bitcast.97, bf16[256,8,5,256]{3,0,2,1:T(8,128)(2,1)} %all-gather.6.cloned.1.call-done), kind=kOutput, calls=%fused_computation.39 | convolution fusion | flops 671350784 | bytes 8388608 | tf_op jit(solution)/shard_map/tckd,fckd->tcf/dot_general | solution.py:75
  107.4 1.1 copy.47
  108.4 1.3 reshape.188
  109.8 2.1 collective-permute-start
  111.9 3.4 collective-permute-start.1
  115.4 2.0 collective-permute-done
  117.5 3.3 collective-permute-done.1
  120.9 0.9 fusion.25
  121.8 1.3 copy.70
  123.1 26.4 %all-gather.8.cloned.1.call-done = bf16[256,8,5,256]{3,0,2,1:T(8,128)(2,1)} async-done(((bf16[16,8,5,256]{3,0,2,1:T(8,128)(2,1)}), bf16[256,8,5,256]{3,0,2,1:T(8,128)(2,1)}) %all-gather.8.cloned.1.call-update) | async-done | bytes 5242896 | tf_op jit(solution)/shard_map/all_gather | solution.py:36
  149.5 5.1 %multiply_convert_fusion = (bf16[128,8,256]{2,0,1:T(8,128)(2,1)S(1)}, bf16[128,8,256]{2,0,1:T(8,128)(2,1)}) fusion(f32[128,8,256]{2,1,0:T(8,128)} %bitcast.107, bf16[128,8,5,256]{3,0,2,1:T(8,128)(2,1)S(1)} %bitcast.99, bf16[256,8,5,256]{3,0,2,1:T(8,128)(2,1)} %all-gather.8.cloned.1.call-done), kind=kOutput, calls=%fused_computation.76 | convolution fusion | flops 676593664 | bytes 9961472 | tf_op jit(solution)/shard_map/tckb,bcke->tce/dot_general | solution.py:70
  154.7 1.1 copy.54
  155.7 2.1 reshape.192
  157.8 1.1 fusion.46
  158.9 2.1 collective-permute-start.2
  161.1 3.6 %collective-permute-start.3 = (bf16[1,1,64,2048]{3,2,1,0:T(8,128)(2,1)S(1)}, bf16[1,1,64,2048]{3,2,1,0:T(8,128)(2,1)S(1)}, u32[]{:S(2)}, u32[]{:S(2)}) collective-permute-start(bf16[1,1,64,2048]{3,2,1,0:T(8,128)(2,1)S(1)} %get-tuple-element.31), channel_id=1, source_target_pairs={{8,0},{16,8},{24,16},{32,24},{40,32},{48,40},{56,48},{64,56},{72,6... | collective-permute-start | bytes 786440 | tf_op jit(solution)/shard_map/ppermute | solution.py:19
  164.7 2.7 convolution_bitcast_fusion.1
  167.3 1.0 collective-permute-done.3
  168.5 0.9 add_convert_fusion
  169.5 0.7 copy-done.1
  170.3 1.6 convolution_bitcast_fusion
  171.8 5.7 %fusion = bf16[256,2,8,5,256]{0,4,3,2,1:T(8,128)(2,1)} fusion(f32[256,1,8,5,256]{0,4,3,2,1:T(8,128)S(1)} %convolution_bitcast_fusion, f32[256,1,8,5,256]{0,4,3,2,1:T(8,128)S(1)} %convolution_bitcast_fusion.1), kind=kLoop, calls=%fused_computation.3 | loop fusion | flops 15728640 | bytes 31457280 | tf_op jit(solution)/shard_map/convert_element_type | solution.py:122
  177.5 15.4 %copy.57 = bf16[256,2,8,5,256]{4,2,3,1,0:T(8,128)(2,1)} copy(bf16[256,2,8,5,256]{0,4,3,2,1:T(8,128)(2,1)} %fusion) | data formatting | bytes 20971520 | tf_op jit(solution)/shard_map/convert_element_type | solution.py:122
  193.0 0.9 copy-done.4
  193.9 4.3 %convolution_bitcast_fusion.2 = f32[128,8,5,256]{3,0,2,1:T(8,128)S(1)} fusion(bf16[256,8,5,256]{3,0,2,1:T(8,128)(2,1)} %all-gather.8.cloned.1.call-done, bf16[128,8,256]{2,0,1:T(8,128)(2,1)S(1)} %copy-done.4), kind=kOutput, calls=%fused_computation.19 | convolution fusion | flops 671088640 | bytes 11010048 | tf_op jit(solution)/shard_map/tce,bcke->tckb/dot_general | solution.py:103
  198.2 5.8 %fusion.5 = bf16[128,16,256]{2,1,0:T(8,128)(2,1)} fusion(f32[128,8,5,256]{3,0,2,1:T(8,128)S(1)} %convolution_bitcast_fusion.2, s32[8,5]{0,1:T(8,128)S(1)} %copy.44), kind=kOutput, calls=%fused_computation.35 | convolution fusion | flops 252183168 | bytes 6291616 | tf_op jit(solution)/shard_map/tckb,ckr->trb/dot_general | solution.py:109
  204.0 2.3 convert_element_type.87
  206.4 1.0 fusion.39
  207.6 117.1 %psum.7 = bf16[9,2048]{1,0:T(8,128)(2,1)S(1)} all-reduce(bf16[9,2048]{1,0:T(8,128)(2,1)S(1)} %multiply_convert_fusion.1), channel_id=1, replica_groups=mesh['crop'=2,'rows'=16,'hid'=8] {'crop','rows'}, use_global_device_ids=true, to_apply=%region_11.13 | all-reduce | flops 18432 | bytes 73728 | tf_op jit(solution)/shard_map/psum | solution.py:102
  324.7 0.7 convert_element_type.95
  325.4 1.0 convert_element_type.92
  326.4 0.9 slice_bitcast_fusion
  327.3 17.5 %reduce-scatter.3.cloned.1.call-done = bf16[1,2,64,512]{3,2,1,0:T(8,128)(2,1)} async-done(((bf16[1,2,64,4096]{3,2,1,0:T(8,128)(2,1)}), bf16[1,2,64,512]{3,2,1,0:T(8,128)(2,1)}) %reduce-scatter.3.cloned.1.call-update) | async-done | bytes 131088 | tf_op jit(solution)/shard_map/reduce_scatter | solution.py:112
  (36 shorter events, 1.2 us)
Async XLA Ops:
  7.2 53.0 %all-gather.4.cloned.1.call-start = ((), (), s32[]{:S(2)}) async-start(), calls=%async_computation.3 | async-start | bytes 1179648 | tf_op jit(solution)/shard_map/all_gather | solution.py:54
  7.9 14.2 %copy-start.6 = (s32[8,5]{1,0:T(8,128)S(1)}, s32[8,5]{1,0:T(8,128)}, u32[]{:S(2)}) copy-start(s32[8,5]{1,0:T(8,128)} %param.13) | copy-start | bytes 484
  7.9 95.1 %all-gather.6.cloned.1.call-start = ((), (), s32[]{:S(2)}) async-start(), calls=%async_computation.4 | async-start | bytes 5570560 | tf_op jit(solution)/shard_map/all_gather | solution.py:37
  9.7 139.8 %all-gather.8.cloned.1.call-start = ((), (), s32[]{:S(2)}) async-start(), calls=%async_computation.5 | async-start | bytes 5570560 | tf_op jit(solution)/shard_map/all_gather | solution.py:36
  13.6 48.4 %all-to-all-start = ((bf16[8,1,2,64,512]{4,3,2,1,0:T(8,128)(2,1)}), bf16[8,1,2,64,512]{4,3,2,1,0:T(8,128)(2,1)S(1)}, u32[]{:S(2)}, u32[]{:S(2)}) async-start(bf16[8,1,2,64,512]{4,3,2,1,0:T(8,128)(2,1)} %stack.50), calls=%async_computation | async-start | bytes 2097152 | tf_op jit(solution)/shard_map/all_to_all | solution.py:42
  22.0 303.4 %reduce-scatter.5.cloned.1.call-start = ((), (), s32[]{:S(2)}) async-start(), calls=%async_computation.7 | async-start | bytes 10813440 | tf_op jit(solution)/shard_map/reduce_scatter | solution.py:121
  74.8 32.5 %copy-start = (bf16[40,128,256]{2,1,0:T(8,128)(2,1)}, bf16[40,128,256]{2,1,0:T(8,128)(2,1)S(1)}, u32[]{:S(2)}) copy-start(bf16[40,128,256]{2,1,0:T(8,128)(2,1)S(1)} %get-tuple-element.43) | copy-start | bytes 7864324
  107.3 8.0 %copy-start.5 = (f32[9,2048]{1,0:T(8,128)S(1)}, f32[9,2048]{1,0:T(8,128)}, u32[]{:S(2)}) copy-start(f32[9,2048]{1,0:T(8,128)} %param.12) | copy-start | bytes 221188
  109.8 7.7 %collective-permute-start = (bf16[1,1,64,2048]{3,2,1,0:T(8,128)(2,1)S(1)}, bf16[1,1,64,2048]{3,2,1,0:T(8,128)(2,1)S(1)}, u32[]{:S(2)}, u32[]{:S(2)}) collective-permute-start(bf16[1,1,64,2048]{3,2,1,0:T(8,128)(2,1)S(1)} %get-tuple-element.32), channel_id=1, source_target_pairs={{0,8},{8,16},{16,24},{24,32},{32,40},{40,48},{48,56},{56,64},{64,7... | collective-permute-start | bytes 786440 | tf_op jit(solution)/shard_map/ppermute | solution.py:18
  111.9 8.8 %collective-permute-start.1 = (bf16[1,1,64,2048]{3,2,1,0:T(8,128)(2,1)S(1)}, bf16[1,1,64,2048]{3,2,1,0:T(8,128)(2,1)S(1)}, u32[]{:S(2)}, u32[]{:S(2)}) collective-permute-start(bf16[1,1,64,2048]{3,2,1,0:T(8,128)(2,1)S(1)} %get-tuple-element.33), channel_id=1, source_target_pairs={{8,0},{16,8},{24,16},{32,24},{40,32},{48,40},{56,48},{64,56},{72,6... | collective-permute-start | bytes 786440 | tf_op jit(solution)/shard_map/ppermute | solution.py:19
  120.9 28.6 %copy-start.2 = (bf16[40,128,256]{2,1,0:T(8,128)(2,1)S(1)}, bf16[40,128,256]{2,1,0:T(8,128)(2,1)}, u32[]{:S(2)}) copy-start(bf16[40,128,256]{2,1,0:T(8,128)(2,1)} %get-tuple-element.44) | copy-start | bytes 7864324
  158.9 8.4 %collective-permute-start.2 = (bf16[1,1,64,2048]{3,2,1,0:T(8,128)(2,1)S(1)}, bf16[1,1,64,2048]{3,2,1,0:T(8,128)(2,1)S(1)}, u32[]{:S(2)}, u32[]{:S(2)}) collective-permute-start(bf16[1,1,64,2048]{3,2,1,0:T(8,128)(2,1)S(1)} %get-tuple-element.30), channel_id=1, source_target_pairs={{0,8},{8,16},{16,24},{24,32},{32,40},{40,48},{48,56},{56,64},{64,7... | collective-permute-start | bytes 786440 | tf_op jit(solution)/shard_map/ppermute | solution.py:18
  161.1 7.3 %collective-permute-start.3 = (bf16[1,1,64,2048]{3,2,1,0:T(8,128)(2,1)S(1)}, bf16[1,1,64,2048]{3,2,1,0:T(8,128)(2,1)S(1)}, u32[]{:S(2)}, u32[]{:S(2)}) collective-permute-start(bf16[1,1,64,2048]{3,2,1,0:T(8,128)(2,1)S(1)} %get-tuple-element.31), channel_id=1, source_target_pairs={{8,0},{16,8},{24,16},{32,24},{40,32},{48,40},{56,48},{64,56},{72,6... | collective-permute-start | bytes 786440 | tf_op jit(solution)/shard_map/ppermute | solution.py:19
  164.7 3.7 %copy-start.3 = (bf16[1,2,64,2048]{3,2,1,0:T(8,128)(2,1)S(1)}, bf16[1,2,64,2048]{3,2,1,0:T(8,128)(2,1)}, u32[]{:S(2)}) copy-start(bf16[1,2,64,2048]{3,2,1,0:T(8,128)(2,1)} %reshape.192) | copy-start | bytes 1572868
  168.5 1.7 copy-start.1
  192.8 1.0 copy-start.4
  192.9 151.9 %reduce-scatter.3.cloned.1.call-start = ((), (), s32[]{:S(2)}) async-start(), calls=%async_computation.6 | async-start | bytes 1179648 | tf_op jit(solution)/shard_map/reduce_scatter | solution.py:112
Sparse Core Ops, SparseCore 0:
  9.8 50.3 all-gather.3
  62.6 40.4 all-gather.5
  105.4 44.0 all-gather.7
  193.0 110.1 reduce-scatter.4
  306.4 38.3 reduce-scatter.2
